TPU v7x, 512 devices: a whole 4x4x16 slice. The times are simulated.
512 devices in a mesh: mesh: 64 (over y, z), obs: 8 (over x, core).
Axes of the slice: x: 4, y: 4, z: 16, core: 2. Of those that a mesh axis runs over, the one named last changes fastest.
Arguments:
- probes: bfloat16 [64, 512, 2048], P(None, 'mesh', 'obs'), may hold values from -6 to 6
- velocity: float32 [512, 2048], P('mesh', 'obs'), may hold values from 0.5 to 2
- viscosity: float32 [512, 2048], P('mesh', 'obs'), may hold values from 0.1 to 3
- friction: float32 [512, 2048], P('mesh', 'obs'), may hold values from 0.5 to 4
- obs_block: int32 [64, 512], P('mesh', 'obs'), may hold values from 0 to 127
- obs_weight: float32 [64, 512, 128], P('mesh', 'obs'), may hold values from -0.5 to 0.5
- obs_prec: float32 [64, 512], P('mesh', 'obs'), may hold values from 0.05 to 0.5
- rank: int32 [1], replicated, may hold values from 1 to 64
Outputs:
- basis: float32 [64, 512, 2048], P(None, 'mesh', 'obs')
- factor: float32 [64, 64], replicated
All inputs are finite; a program needn't handle non-finite values.
Results may differ from a plain program's by a relative error of at most 0.0027.
Values may be sent and summed in bfloat16 or wider, within the bound.
A program may use at most 64 MiB of HBM per device.

v0:
```python
import jax
import jax.numpy as jnp
from jax import lax
from jax.sharding import PartitionSpec as P

BLOCK = 128
PRIOR = 1.0


def extended(block, sides, width):
    for axis, dim in sides:
        count = lax.axis_size(axis)
        forward = [(i, i + 1) for i in range(count - 1)]
        backward = [(target, source) for source, target in forward]
        low = lax.ppermute(
            lax.slice_in_dim(block, block.shape[dim] - width, None, axis=dim), axis, forward
        )
        high = lax.ppermute(lax.slice_in_dim(block, 0, width, axis=dim), axis, backward)
        block = jnp.concatenate([low, block, high], axis=dim)
    return block


def apply_padded(padded, visc_pad, friction):
    height = padded.shape[1] - 2
    width = padded.shape[2] - 2
    centre = padded[:, 1:-1, 1:-1]
    visc_mid = visc_pad[1:-1, 1:-1]
    result = friction * centre
    for shift_row, shift_col in ((2, 1), (0, 1), (1, 2), (1, 0)):
        neighbor = padded[:, shift_row : shift_row + height, shift_col : shift_col + width]
        face_coef = 0.5 * (
            visc_mid + visc_pad[shift_row : shift_row + height, shift_col : shift_col + width]
        )
        result = result + face_coef * (centre - neighbor)
    return result


def per_device(probes, velocity, viscosity, friction, obs_block, obs_weight, obs_prec, rank):
    probe_count = probes.shape[0]
    rows_here, cols_here = velocity.shape
    obs_devices = lax.axis_size("obs")
    slab_columns = cols_here * obs_devices // BLOCK
    owned_blocks = cols_here // BLOCK
    cell_total = rows_here * cols_here * lax.axis_size("mesh") * obs_devices
    omega = probes.astype(jnp.float32)
    stacked = jnp.concatenate([velocity[None] * omega, viscosity[None]], axis=0)
    padded = extended(stacked, (("mesh", 1), ("obs", 2)), 1)
    visc_pad = padded[-1]
    tangent = apply_padded(padded[:-1], visc_pad, friction).astype(jnp.bfloat16)
    row_ids = obs_block[0] // slab_columns
    col_ids = obs_block[0] % slab_columns
    weights = obs_weight[0]
    precision = obs_prec[0]
    segment = lax.all_gather(tangent, "obs", axis=2, tiled=True)
    seg_blocks = segment.shape[2] // BLOCK
    local_col = col_ids
    inside = (local_col >= 0) & (local_col < seg_blocks)
    block_index = row_ids * seg_blocks + jnp.clip(local_col, 0, seg_blocks - 1)
    blocks = segment.reshape(probe_count, rows_here * seg_blocks, BLOCK)
    picked = jnp.take(blocks, block_index, axis=1).astype(jnp.float32)
    value = precision * jnp.sum(picked * weights, axis=-1)
    misfit = jnp.where(inside, value, 0.0)
    amount = lax.axis_size("obs") * owned_blocks
    local_col = col_ids
    inside = (local_col >= 0) & (local_col < amount)
    block_index = jnp.clip(local_col, 0, amount - 1) * rows_here + row_ids
    contrib = jnp.where(inside[None, :, None], misfit[:, :, None] * weights[None], 0.0)
    partial_value = (
        jnp.zeros((probe_count, amount * rows_here, BLOCK), jnp.float32)
        .at[:, block_index]
        .add(contrib)
    )
    received = lax.psum_scatter(
        partial_value.reshape(probe_count, amount, rows_here, BLOCK).transpose(1, 0, 2, 3),
        "obs",
        scatter_dimension=0,
        tiled=True,
    )
    source = received.transpose(1, 2, 0, 3).reshape(probe_count, rows_here, cols_here)
    padded_source = extended(source, (("mesh", 1), ("obs", 2)), 1)
    gradient = velocity * apply_padded(padded_source, visc_pad, friction)
    sketch = (gradient + PRIOR * omega).reshape(probe_count, rows_here * cols_here)
    local_gram = (
        jnp.dot(
            sketch, sketch.T, precision=lax.Precision.HIGHEST, preferred_element_type=jnp.float32
        )
        / cell_total
    )
    factor = jnp.linalg.cholesky(lax.psum(local_gram, ("mesh", "obs")))
    solved = lax.linalg.triangular_solve(factor, sketch, left_side=True, lower=True)
    retained = (jnp.arange(probe_count, dtype=jnp.int32) < rank[0])[:, None]
    basis = jnp.where(retained, solved, 0.0).reshape(probe_count, rows_here, cols_here)
    return (basis, factor)


def solution(mesh):
    in_specs = (
        P(None, "mesh", "obs"),
        P("mesh", "obs"),
        P("mesh", "obs"),
        P("mesh", "obs"),
        P("mesh", "obs"),
        P("mesh", "obs", None),
        P("mesh", "obs"),
        P(),
    )
    out_specs = (P(None, "mesh", "obs"), P())
    return jax.shard_map(
        per_device, mesh=mesh, in_specs=in_specs, out_specs=out_specs, check_vma=False
    )
```

profile of v0, /device:TPU:1, one launch (start us, length us, event | category | flops | bytes accessed | tf_op | source)
XLA Modules:
  0.0 289.0 jit_solution(15032128486639405339)
XLA Ops:
  7.2 0.0 all-gather.2.cloned.1.call-start
  7.2 1.0 convert_multiply_fusion
  8.2 0.9 pad_maximum_fusion.23
  9.1 4.4 %collective-permute-start = (f32[65,1,256]{2,0,1:T(8,128)S(1)}, f32[65,1,256]{2,0,1:T(8,128)S(1)}, u32[]{:S(2)}, u32[]{:S(2)}) collective-permute-start(f32[65,1,256]{2,0,1:T(8,128)S(1)} %copy.38), channel_id=1, source_target_pairs={{0,8},{8,16},{16,24},{24,32},{32,40},{40,48},{48,56},{56,64},{64,7... | collective-permute-start | bytes 199688 | tf_op jit(solution)/shard_map/ppermute | solution.py:15
  13.5 1.3 collective-permute-start.1
  14.8 0.1 collective-permute-done
  14.9 0.1 copy.40
  14.9 3.8 %collective-permute-done.1 = f32[65,1,256]{2,0,1:T(8,128)S(1)} collective-permute-done((f32[65,1,256]{2,0,1:T(8,128)S(1)}, f32[65,1,256]{2,0,1:T(8,128)S(1)}, u32[]{:S(2)}, u32[]{:S(2)}) %collective-permute-start.1) | collective-permute-done | bytes 66592 | tf_op jit(solution)/shard_map/ppermute | solution.py:18
  18.8 0.1 copy.41
  18.8 0.9 pad_maximum_fusion
  19.7 0.0 copy-start.2
  19.7 0.2 fusion.39
  19.9 0.0 copy-start.4
  20.0 0.3 copy.42
  20.2 4.9 %collective-permute-start.2 = (f32[65,10,1]{0,1,2:T(8,128)S(1)}, f32[65,10,1]{0,1,2:T(8,128)S(1)}, u32[]{:S(2)}, u32[]{:S(2)}) collective-permute-start(f32[65,10,1]{0,1,2:T(8,128)S(1)} %copy.42), channel_id=1, source_target_pairs={{0,1},{1,2},{2,3},{3,4},{4,5},{5,6},{6,7},{8,9},{9,10},{10,11},{11... | collective-permute-start | bytes 7808 | tf_op jit(solution)/shard_map/ppermute | solution.py:15
  25.2 0.3 copy.43
  25.4 3.0 %collective-permute-start.3 = (f32[65,10,1]{0,1,2:T(8,128)S(1)}, f32[65,10,1]{0,1,2:T(8,128)S(1)}, u32[]{:S(2)}, u32[]{:S(2)}) collective-permute-start(f32[65,10,1]{0,1,2:T(8,128)S(1)} %copy.43), channel_id=1, source_target_pairs={{1,0},{2,1},{3,2},{4,3},{5,4},{6,5},{7,6},{9,8},{10,9},{11,10},{12... | collective-permute-start | bytes 7808 | tf_op jit(solution)/shard_map/ppermute | solution.py:18
  28.5 0.0 collective-permute-done.2
  28.5 0.3 copy.44
  28.8 1.6 collective-permute-done.3
  30.4 0.3 copy.45
  30.8 0.0 copy-done.2
  30.8 0.0 copy-start.6
  30.8 0.1 fusion.30
  30.9 0.1 fusion.34
  30.9 1.8 fusion.17
  32.7 0.0 all-gather.2.cloned.1.call-update
  32.7 0.0 reduce-scatter.2.cloned.1.call-start
  32.9 38.9 %all-gather.2.cloned.1.call-done = bf16[64,8,2048]{2,1,0:T(8,128)(2,1)} async-done(((bf16[64,8,256]{2,1,0:T(8,128)(2,1)}), bf16[64,8,2048]{2,1,0:T(8,128)(2,1)}) %all-gather.2.cloned.1.call-update) | async-done | bytes 2097168 | tf_op jit(solution)/shard_map/all_gather | solution.py:54
  71.7 2.9 reshape.238
  74.6 2.7 copy.50
  77.3 2.3 gather_fusion
  79.6 0.9 multiply_reduce_fusion
  80.5 0.1 select_bitcast_fusion.1
  80.6 0.8 select_bitcast_fusion
  81.4 2.5 broadcast_in_dim.67
  83.9 9.0 %scatter_fusion = f32[64,128,128]{2,0,1:T(8,128)} fusion(f32[64,128,128]{2,0,1:T(8,128)} %broadcast_in_dim.67, s32[64]{0:T(128)S(1)} %fusion.36, f32[64,64,128]{2,1,0:T(8,128)S(1)} %select_bitcast_fusion), kind=kCustom, calls=%fused_computation.1 | custom fusion | flops 524288 | bytes 6291712 | tf_op jit(solution)/shard_map/scatter-add | solution.py:71
  92.9 0.0 reduce-scatter.2.cloned.1.call-update
  92.9 44.1 %reduce-scatter.2.cloned.1.call-done = f32[2,64,8,128]{3,1,2,0:T(8,128)} async-done(((f32[16,64,8,128]{3,1,2,0:T(8,128)}), f32[2,64,8,128]{3,1,2,0:T(8,128)}) %reduce-scatter.2.cloned.1.call-update) | async-done | bytes 524304 | tf_op jit(solution)/shard_map/reduce_scatter | solution.py:73
  137.0 1.3 copy.63
  138.3 0.0 copy-start
  138.4 0.0 copy-start.3
  138.4 0.1 fusion.41
  138.5 1.3 collective-permute-start.4
  139.8 4.0 %collective-permute-start.5 = (f32[64,1,256]{2,1,0:T(1,128)S(1)}, f32[64,1,256]{2,1,0:T(1,128)S(1)}, u32[]{:S(2)}, u32[]{:S(2)}) collective-permute-start(f32[64,1,256]{2,1,0:T(1,128)S(1)} %get-tuple-element.13), channel_id=1, source_target_pairs={{0,8},{8,16},{16,24},{24,32},{32,40},{40,48},{48,56},{56,64},{64,7... | collective-permute-start | bytes 196616 | tf_op jit(solution)/shard_map/ppermute | solution.py:15
  144.4 0.0 collective-permute-done.4
  144.4 0.7 collective-permute-done.5
  145.1 0.2 pad_maximum_fusion.1
  145.3 0.2 fusion.40
  145.5 6.2 %collective-permute-start.6 = (f32[64,10,1]{2,1,0:T(8,128)S(1)}, f32[64,10,1]{2,1,0:T(8,128)S(1)}, u32[]{:S(2)}, u32[]{:S(2)}) collective-permute-start(f32[64,10,1]{2,1,0:T(8,128)S(1)} %get-tuple-element.9), channel_id=1, source_target_pairs={{1,0},{2,1},{3,2},{4,3},{5,4},{6,5},{7,6},{9,8},{10,9},{11,10},{12... | collective-permute-start | bytes 7688 | tf_op jit(solution)/shard_map/ppermute | solution.py:18
  151.6 1.9 collective-permute-start.7
  153.6 2.5 collective-permute-done.6
  156.1 3.6 %collective-permute-done.7 = f32[64,10,1]{2,1,0:T(8,128)S(1)} collective-permute-done((f32[64,10,1]{2,1,0:T(8,128)S(1)}, f32[64,10,1]{2,1,0:T(8,128)S(1)}, u32[]{:S(2)}, u32[]{:S(2)}) %collective-permute-start.7) | collective-permute-done | bytes 2592 | tf_op jit(solution)/shard_map/ppermute | solution.py:15
  159.7 0.8 convert_add_fusion
  160.5 0.7 fusion
  161.2 106.3 %psum.7 = f32[64,64]{0,1:T(8,128)S(1)} all-reduce(f32[64,64]{0,1:T(8,128)S(1)} %fusion), channel_id=1, replica_groups=mesh['mesh'=64,'obs'=8] {'mesh','obs'}, use_global_device_ids=true, to_apply=%region_3.4 | all-reduce | flops 4096 | bytes 32768 | tf_op jit(solution)/shard_map/psum | solution.py:89
  267.6 0.1 copy.55
  267.7 5.8 %cholesky.15 = f32[64,64]{1,0:T(8,128)S(1)} custom-call(f32[64,64]{1,0:T(8,128)S(1)} %fusion.29), custom_call_target="Cholesky" | custom-call | tf_op jit(solution)/shard_map/jit(cholesky)/cholesky | solution.py:89
  273.5 0.6 compare_reduce_fusion
  274.2 1.3 select_bitcast_fusion.2
  275.4 4.9 %custom-call.6 = f32[1,64,64]{1,2,0:T(8,128)S(1)} custom-call(f32[1,64,64]{2,1,0:T(8,128)S(1)} %get-tuple-element.2), custom_call_target="InvertDiagBlocksLowerTriangular" | custom-call | tf_op jit(solution)/shard_map/triangular_solve | solution.py:90
  280.3 0.2 copy.58
  280.5 0.6 convolution_select_fusion
  281.2 1.0 copy.59
  (17 shorter events, 0.1 us)
Async XLA Ops:
  7.2 64.5 %all-gather.2.cloned.1.call-start = ((), (), s32[]{:S(2)}) async-start(), calls=%async_computation.1 | async-start | bytes 2359296 | tf_op jit(solution)/shard_map/all_gather | solution.py:54
  9.1 5.8 %collective-permute-start = (f32[65,1,256]{2,0,1:T(8,128)S(1)}, f32[65,1,256]{2,0,1:T(8,128)S(1)}, u32[]{:S(2)}, u32[]{:S(2)}) collective-permute-start(f32[65,1,256]{2,0,1:T(8,128)S(1)} %copy.38), channel_id=1, source_target_pairs={{0,8},{8,16},{16,24},{24,32},{32,40},{40,48},{48,56},{56,64},{64,7... | collective-permute-start | bytes 199688 | tf_op jit(solution)/shard_map/ppermute | solution.py:15
  13.5 5.3 %collective-permute-start.1 = (f32[65,1,256]{2,0,1:T(8,128)S(1)}, f32[65,1,256]{2,0,1:T(8,128)S(1)}, u32[]{:S(2)}, u32[]{:S(2)}) collective-permute-start(f32[65,1,256]{2,0,1:T(8,128)S(1)} %copy.39), channel_id=1, source_target_pairs={{8,0},{16,8},{24,16},{32,24},{40,32},{48,40},{56,48},{64,56},{72,6... | collective-permute-start | bytes 199688 | tf_op jit(solution)/shard_map/ppermute | solution.py:18
  19.7 11.0 %copy-start.2 = (f32[8,256]{1,0:T(8,128)S(1)}, f32[8,256]{1,0:T(8,128)}, u32[]{:S(2)}) copy-start(f32[8,256]{1,0:T(8,128)} %param.10) | copy-start | bytes 24580
  19.9 11.0 %copy-start.4 = (f32[8,256]{1,0:T(8,128)S(1)}, f32[8,256]{1,0:T(8,128)}, u32[]{:S(2)}) copy-start(f32[8,256]{1,0:T(8,128)} %param.11) | copy-start | bytes 24580
  20.2 8.2 %collective-permute-start.2 = (f32[65,10,1]{0,1,2:T(8,128)S(1)}, f32[65,10,1]{0,1,2:T(8,128)S(1)}, u32[]{:S(2)}, u32[]{:S(2)}) collective-permute-start(f32[65,10,1]{0,1,2:T(8,128)S(1)} %copy.42), channel_id=1, source_target_pairs={{0,1},{1,2},{2,3},{3,4},{4,5},{5,6},{6,7},{8,9},{9,10},{10,11},{11... | collective-permute-start | bytes 7808 | tf_op jit(solution)/shard_map/ppermute | solution.py:15
  25.4 5.0 %collective-permute-start.3 = (f32[65,10,1]{0,1,2:T(8,128)S(1)}, f32[65,10,1]{0,1,2:T(8,128)S(1)}, u32[]{:S(2)}, u32[]{:S(2)}) collective-permute-start(f32[65,10,1]{0,1,2:T(8,128)S(1)} %copy.43), channel_id=1, source_target_pairs={{1,0},{2,1},{3,2},{4,3},{5,4},{6,5},{7,6},{9,8},{10,9},{11,10},{12... | collective-permute-start | bytes 7808 | tf_op jit(solution)/shard_map/ppermute | solution.py:18
  30.8 2.0 copy-start.6
  32.7 104.3 %reduce-scatter.2.cloned.1.call-start = ((), (), s32[]{:S(2)}) async-start(), calls=%async_computation.2 | async-start | bytes 4718592 | tf_op jit(solution)/shard_map/reduce_scatter | solution.py:73
  77.3 2.4 copy-start.1
  77.3 3.2 %copy-start.5 = (f32[1,64]{1,0:T(1,128)S(1)}, f32[1,64]{1,0:T(1,128)}, u32[]{:S(2)}) copy-start(f32[1,64]{1,0:T(1,128)} %param.14) | copy-start | bytes 772
  138.3 21.3 %copy-start = (bf16[64,8,256]{2,1,0:T(8,128)(2,1)S(1)}, bf16[64,8,256]{2,1,0:T(8,128)(2,1)}, u32[]{:S(2)}) copy-start(bf16[64,8,256]{2,1,0:T(8,128)(2,1)} %param.8) | copy-start | bytes 786436
  138.4 21.3 %copy-start.3 = (f32[8,256]{1,0:T(8,128)S(1)}, f32[8,256]{1,0:T(8,128)}, u32[]{:S(2)}) copy-start(f32[8,256]{1,0:T(8,128)} %param.9) | copy-start | bytes 24580
  138.5 5.9 %collective-permute-start.4 = (f32[64,1,256]{2,1,0:T(1,128)S(1)}, f32[64,1,256]{2,1,0:T(1,128)S(1)}, u32[]{:S(2)}, u32[]{:S(2)}) collective-permute-start(f32[64,1,256]{2,1,0:T(1,128)S(1)} %get-tuple-element.14), channel_id=1, source_target_pairs={{8,0},{16,8},{24,16},{32,24},{40,32},{48,40},{56,48},{64,56},{72,6... | collective-permute-start | bytes 196616 | tf_op jit(solution)/shard_map/ppermute | solution.py:18
  139.8 5.3 %collective-permute-start.5 = (f32[64,1,256]{2,1,0:T(1,128)S(1)}, f32[64,1,256]{2,1,0:T(1,128)S(1)}, u32[]{:S(2)}, u32[]{:S(2)}) collective-permute-start(f32[64,1,256]{2,1,0:T(1,128)S(1)} %get-tuple-element.13), channel_id=1, source_target_pairs={{0,8},{8,16},{16,24},{24,32},{32,40},{40,48},{48,56},{56,64},{64,7... | collective-permute-start | bytes 196616 | tf_op jit(solution)/shard_map/ppermute | solution.py:15
  145.5 10.6 %collective-permute-start.6 = (f32[64,10,1]{2,1,0:T(8,128)S(1)}, f32[64,10,1]{2,1,0:T(8,128)S(1)}, u32[]{:S(2)}, u32[]{:S(2)}) collective-permute-start(f32[64,10,1]{2,1,0:T(8,128)S(1)} %get-tuple-element.9), channel_id=1, source_target_pairs={{1,0},{2,1},{3,2},{4,3},{5,4},{6,5},{7,6},{9,8},{10,9},{11,10},{12... | collective-permute-start | bytes 7688 | tf_op jit(solution)/shard_map/ppermute | solution.py:18
  151.6 8.0 %collective-permute-start.7 = (f32[64,10,1]{2,1,0:T(8,128)S(1)}, f32[64,10,1]{2,1,0:T(8,128)S(1)}, u32[]{:S(2)}, u32[]{:S(2)}) collective-permute-start(f32[64,10,1]{2,1,0:T(8,128)S(1)} %get-tuple-element.10), channel_id=1, source_target_pairs={{0,1},{1,2},{2,3},{3,4},{4,5},{5,6},{6,7},{8,9},{9,10},{10,11},{11... | collective-permute-start | bytes 7688 | tf_op jit(solution)/shard_map/ppermute | solution.py:15
Sparse Core Ops, SparseCore 0:
  32.8 38.8 all-gather.1
  93.0 43.9 reduce-scatter.1
where the time goes:
time: 290 us; the launch traced here: 289 us
  blocking collectives  106 us (37%)
  waiting for transfers between devices  95.2 us (33%)
  other arithmetic  29.1 us (10%)
  starting transfers between devices  27 us (9%)
  between operations  15 us (5%)
  local copies, waits for them, and re-layouts  14.9 us (5%)
    psum x1, blocking collectives, per_device(): factor = jnp.linalg.cholesky(lax.psum(local_gram, ('mesh', 'obs')))  106 us
    reduce_scatter x1, waiting for transfers between devices, per_device(): lax.psum_scatter(partial_value.reshape(probe_count, amount, rows_here, BL...  44.1 us
    all_gather x1, waiting for transfers between devices, per_device(): segment = lax.all_gather(tangent, 'obs', axis=2, tiled=True)  38.9 us
    ppermute x4, starting transfers between devices, extended(): lax.ppermute(lax.slice_in_dim(block, block.shape[dim] - width, None, axis...  15.2 us
    ppermute x4, starting transfers between devices, extended(): lax.ppermute(lax.slice_in_dim(block, 0, width, axis=dim), axis, backward)  11.8 us
    scatter-add x1, other arithmetic, per_device(): partial_value = jnp.zeros((probe_count, amount * rows_here, BLOCK), jnp.f...  9.02 us
    ppermute x4, waiting for transfers between devices, extended(): lax.ppermute(lax.slice_in_dim(block, 0, width, axis=dim), axis, backward)  7.92 us
    another operation x3, other arithmetic, per_device(): factor = jnp.linalg.cholesky(lax.psum(local_gram, ('mesh', 'obs')))  6.52 us
  transfers between devices with their start and end apart: 10, of which 8 were waited for; matrix products, arithmetic and copies ran while one was open for 0% of the time, Pallas kernels for 0%

commit v1 on v0

--- a/solution.py
+++ b/solution.py
@@ -86,7 +86,7 @@
         )
         / cell_total
     )
-    factor = jnp.linalg.cholesky(lax.psum(local_gram, ("mesh", "obs")))
+    factor = jnp.linalg.cholesky(jnp.sum(lax.all_gather(local_gram, ("mesh", "obs")), axis=0))
     solved = lax.linalg.triangular_solve(factor, sketch, left_side=True, lower=True)
     retained = (jnp.arange(probe_count, dtype=jnp.int32) < rank[0])[:, None]
     basis = jnp.where(retained, solved, 0.0).reshape(probe_count, rows_here, cols_here)

time: 290 us -> 414 us (1.43)
  waiting for transfers between devices: 95.2 us -> 318 us
  blocking collectives: 106 us -> 0 us
  other arithmetic: 29.1 us -> 36.2 us
    all_gather x0 -> x1, waiting for transfers between devices: none -> 222 us  [per_device(): lax.all_gather(local_gram, ('mesh', 'obs'))]
    psum x1 -> x0, blocking collectives: 106 us -> none  [per_device(): factor = jnp.linalg.cholesky(lax.psum(local_gram, ('mesh', 'obs')))]
    reduce_sum x0 -> x1, other arithmetic: none -> 6.94 us  [per_device(): jnp.sum(lax.all_gather(local_gram, ('mesh', 'obs')), axis=0)]
  transfers between devices with their start and end apart: 10 -> 11, of which waited for: 8 -> 9; matrix products, arithmetic and copies ran while one was open for 0% -> 0% of each run, Pallas kernels for 0% -> 0%
where the time goes in v1:
time: 414 us; the launch traced here: 413 us
  waiting for transfers between devices  318 us (77%)
  other arithmetic  36.2 us (9%)
  starting transfers between devices  27.1 us (7%)
  local copies, waits for them, and re-layouts  14.9 us (4%)
  between operations  14.7 us (4%)
    all_gather x1, waiting for transfers between devices, per_device(): lax.all_gather(local_gram, ('mesh', 'obs'))  222 us
    reduce_scatter x1, waiting for transfers between devices, per_device(): lax.psum_scatter(partial_value.reshape(probe_count, amount, rows_here, BL...  44 us
    all_gather x1, waiting for transfers between devices, per_device(): segment = lax.all_gather(tangent, 'obs', axis=2, tiled=True)  38.9 us
    ppermute x4, starting transfers between devices, extended(): lax.ppermute(lax.slice_in_dim(block, block.shape[dim] - width, None, axis...  15.4 us
    ppermute x4, starting transfers between devices, extended(): lax.ppermute(lax.slice_in_dim(block, 0, width, axis=dim), axis, backward)  11.6 us
    scatter-add x1, other arithmetic, per_device(): partial_value = jnp.zeros((probe_count, amount * rows_here, BLOCK), jnp.f...  9.17 us
  transfers between devices with their start and end apart: 11, of which 9 were waited for; matrix products, arithmetic and copies ran while one was open for 0% of the time, Pallas kernels for 0%

profile of v1, /device:TPU:1, one launch (start us, length us, event | category | flops | bytes accessed | tf_op | source)
XLA Modules:
  0.0 412.5 jit_solution(4944129748539065643)
XLA Ops:
  7.2 0.0 all-gather.4.cloned.1.call-start
  7.2 1.0 convert_multiply_fusion
  8.2 0.9 pad_maximum_fusion.23
  9.1 4.4 %collective-permute-start = (f32[65,1,256]{2,0,1:T(8,128)S(1)}, f32[65,1,256]{2,0,1:T(8,128)S(1)}, u32[]{:S(2)}, u32[]{:S(2)}) collective-permute-start(f32[65,1,256]{2,0,1:T(8,128)S(1)} %copy.34), channel_id=1, source_target_pairs={{0,8},{8,16},{16,24},{24,32},{32,40},{40,48},{48,56},{56,64},{64,7... | collective-permute-start | bytes 199688 | tf_op jit(solution)/shard_map/ppermute | solution.py:15
  13.5 1.3 collective-permute-start.1
  14.8 0.1 collective-permute-done
  14.9 0.1 copy.36
  14.9 3.8 collective-permute-done.1
  18.8 0.1 copy.37
  18.8 0.9 pad_maximum_fusion
  19.7 0.0 copy-start.2
  19.7 0.2 fusion.39
  20.0 0.3 copy.38
  20.2 4.9 %collective-permute-start.2 = (f32[65,10,1]{0,1,2:T(8,128)S(1)}, f32[65,10,1]{0,1,2:T(8,128)S(1)}, u32[]{:S(2)}, u32[]{:S(2)}) collective-permute-start(f32[65,10,1]{0,1,2:T(8,128)S(1)} %copy.38), channel_id=1, source_target_pairs={{0,1},{1,2},{2,3},{3,4},{4,5},{5,6},{6,7},{8,9},{9,10},{10,11},{11... | collective-permute-start | bytes 7808 | tf_op jit(solution)/shard_map/ppermute | solution.py:15
  25.2 0.3 copy.39
  25.4 3.0 collective-permute-start.3
  28.5 0.0 collective-permute-done.2
  28.5 0.3 copy.40
  28.8 1.6 collective-permute-done.3
  30.4 0.3 copy.41
  30.8 0.0 copy-start.6
  30.8 0.1 fusion.30
  30.9 0.1 fusion.34
  30.9 1.8 fusion.17
  32.7 0.0 all-gather.4.cloned.1.call-update
  32.7 0.0 reduce-scatter.2.cloned.1.call-start
  32.9 38.9 %all-gather.4.cloned.1.call-done = bf16[64,8,2048]{2,1,0:T(8,128)(2,1)} async-done(((bf16[64,8,256]{2,1,0:T(8,128)(2,1)}), bf16[64,8,2048]{2,1,0:T(8,128)(2,1)}) %all-gather.4.cloned.1.call-update) | async-done | bytes 2097168 | tf_op jit(solution)/shard_map/all_gather | solution.py:54
  71.7 2.9 reshape.238
  74.6 2.7 copy.46
  77.3 2.3 gather_fusion
  79.7 0.9 multiply_reduce_fusion
  80.5 0.1 select_bitcast_fusion.1
  80.6 0.8 select_bitcast_fusion
  81.4 2.5 broadcast_in_dim.67
  83.9 9.2 %scatter_fusion = f32[64,128,128]{2,0,1:T(8,128)} fusion(f32[64,128,128]{2,0,1:T(8,128)} %broadcast_in_dim.67, s32[64]{0:T(128)S(1)} %fusion.36, f32[64,64,128]{2,1,0:T(8,128)S(1)} %select_bitcast_fusion), kind=kCustom, calls=%fused_computation.1 | custom fusion | flops 524288 | bytes 6291712 | tf_op jit(solution)/shard_map/scatter-add | solution.py:71
  93.0 0.0 reduce-scatter.2.cloned.1.call-update
  93.1 0.0 all-gather.6.cloned.1.call-start
  93.1 44.0 %reduce-scatter.2.cloned.1.call-done = f32[2,64,8,128]{3,1,2,0:T(8,128)} async-done(((f32[16,64,8,128]{3,1,2,0:T(8,128)}), f32[2,64,8,128]{3,1,2,0:T(8,128)}) %reduce-scatter.2.cloned.1.call-update) | async-done | bytes 524304 | tf_op jit(solution)/shard_map/reduce_scatter | solution.py:73
  137.2 1.3 copy.56
  138.5 0.0 copy-start
  138.5 0.0 copy-start.3
  138.5 0.1 fusion.41
  138.6 1.3 collective-permute-start.4
  139.9 4.0 collective-permute-start.5
  143.9 1.3 collective-permute-done.5
  145.2 0.2 pad_maximum_fusion.1
  145.4 0.2 fusion.40
  145.6 6.0 %collective-permute-start.6 = (f32[64,10,1]{2,1,0:T(8,128)S(1)}, f32[64,10,1]{2,1,0:T(8,128)S(1)}, u32[]{:S(2)}, u32[]{:S(2)}) collective-permute-start(f32[64,10,1]{2,1,0:T(8,128)S(1)} %get-tuple-element.9), channel_id=1, source_target_pairs={{1,0},{2,1},{3,2},{4,3},{5,4},{6,5},{7,6},{9,8},{10,9},{11,10},{12... | collective-permute-start | bytes 7688 | tf_op jit(solution)/shard_map/ppermute | solution.py:18
  151.7 2.1 collective-permute-start.7
  153.8 2.3 collective-permute-done.6
  156.1 3.6 collective-permute-done.7
  159.7 0.8 convert_add_fusion
  160.5 1.3 fusion
  161.8 0.0 all-gather.6.cloned.1.call-update
  162.5 0.2 copy.51
  162.7 222.0 %all-gather.6.cloned.1.call-done = f32[32768,64]{1,0:T(8,128)} async-done(((f32[64,64]{1,0:T(8,128)}), f32[32768,64]{1,0:T(8,128)}) %all-gather.6.cloned.1.call-update) | async-done | bytes 8388624 | tf_op jit(solution)/shard_map/all_gather | solution.py:89
  384.7 6.9 %reduce_sum.19 = f32[64,64]{1,0:T(8,128)S(1)} reduce(f32[512,64,64]{2,1,0:T(8,128)} %bitcast.76, f32[]{:T(128)} %constant.86.clone.1), dimensions={0}, to_apply=%region_3.4 | reduce | flops 2093056 | bytes 8404996 | tf_op jit(solution)/shard_map/reduce_sum | solution.py:89
  391.6 0.1 copy.50
  391.7 5.8 %cholesky.15 = f32[64,64]{1,0:T(8,128)S(1)} custom-call(f32[64,64]{1,0:T(8,128)S(1)} %fusion.29), custom_call_target="Cholesky" | custom-call | tf_op jit(solution)/shard_map/jit(cholesky)/cholesky | solution.py:89
  397.6 0.6 compare_reduce_fusion
  398.2 1.3 select_bitcast_fusion.2
  399.5 4.9 %custom-call.6 = f32[1,64,64]{1,2,0:T(8,128)S(1)} custom-call(f32[1,64,64]{2,1,0:T(8,128)S(1)} %get-tuple-element.2), custom_call_target="InvertDiagBlocksLowerTriangular" | custom-call | tf_op jit(solution)/shard_map/triangular_solve | solution.py:90
  404.4 0.6 convolution_select_fusion
  405.1 1.0 copy.52
  (20 shorter events, 0.1 us)
Async XLA Ops:
  7.2 64.5 %all-gather.4.cloned.1.call-start = ((), (), s32[]{:S(2)}) async-start(), calls=%async_computation.1 | async-start | bytes 2359296 | tf_op jit(solution)/shard_map/all_gather | solution.py:54
  9.1 5.8 %collective-permute-start = (f32[65,1,256]{2,0,1:T(8,128)S(1)}, f32[65,1,256]{2,0,1:T(8,128)S(1)}, u32[]{:S(2)}, u32[]{:S(2)}) collective-permute-start(f32[65,1,256]{2,0,1:T(8,128)S(1)} %copy.34), channel_id=1, source_target_pairs={{0,8},{8,16},{16,24},{24,32},{32,40},{40,48},{48,56},{56,64},{64,7... | collective-permute-start | bytes 199688 | tf_op jit(solution)/shard_map/ppermute | solution.py:15
  13.5 5.3 %collective-permute-start.1 = (f32[65,1,256]{2,0,1:T(8,128)S(1)}, f32[65,1,256]{2,0,1:T(8,128)S(1)}, u32[]{:S(2)}, u32[]{:S(2)}) collective-permute-start(f32[65,1,256]{2,0,1:T(8,128)S(1)} %copy.35), channel_id=1, source_target_pairs={{8,0},{16,8},{24,16},{32,24},{40,32},{48,40},{56,48},{64,56},{72,6... | collective-permute-start | bytes 199688 | tf_op jit(solution)/shard_map/ppermute | solution.py:18
  19.7 11.0 %copy-start.2 = (f32[8,256]{1,0:T(8,128)S(1)}, f32[8,256]{1,0:T(8,128)}, u32[]{:S(2)}) copy-start(f32[8,256]{1,0:T(8,128)} %param.10) | copy-start | bytes 24580
  19.9 11.0 %copy-start.4 = (f32[8,256]{1,0:T(8,128)S(1)}, f32[8,256]{1,0:T(8,128)}, u32[]{:S(2)}) copy-start(f32[8,256]{1,0:T(8,128)} %param.11) | copy-start | bytes 24580
  20.2 8.2 %collective-permute-start.2 = (f32[65,10,1]{0,1,2:T(8,128)S(1)}, f32[65,10,1]{0,1,2:T(8,128)S(1)}, u32[]{:S(2)}, u32[]{:S(2)}) collective-permute-start(f32[65,10,1]{0,1,2:T(8,128)S(1)} %copy.38), channel_id=1, source_target_pairs={{0,1},{1,2},{2,3},{3,4},{4,5},{5,6},{6,7},{8,9},{9,10},{10,11},{11... | collective-permute-start | bytes 7808 | tf_op jit(solution)/shard_map/ppermute | solution.py:15
  25.4 5.0 %collective-permute-start.3 = (f32[65,10,1]{0,1,2:T(8,128)S(1)}, f32[65,10,1]{0,1,2:T(8,128)S(1)}, u32[]{:S(2)}, u32[]{:S(2)}) collective-permute-start(f32[65,10,1]{0,1,2:T(8,128)S(1)} %copy.39), channel_id=1, source_target_pairs={{1,0},{2,1},{3,2},{4,3},{5,4},{6,5},{7,6},{9,8},{10,9},{11,10},{12... | collective-permute-start | bytes 7808 | tf_op jit(solution)/shard_map/ppermute | solution.py:18
  30.8 2.0 copy-start.6
  32.7 104.4 %reduce-scatter.2.cloned.1.call-start = ((), (), s32[]{:S(2)}) async-start(), calls=%async_computation.2 | async-start | bytes 4718592 | tf_op jit(solution)/shard_map/reduce_scatter | solution.py:73
  77.3 2.4 copy-start.1
  77.3 3.2 copy-start.5
  93.1 291.6 %all-gather.6.cloned.1.call-start = ((), (), s32[]{:S(2)}) async-start(), calls=%async_computation.3 | async-start | bytes 16809984 | tf_op jit(solution)/shard_map/all_gather | solution.py:89
  138.5 21.2 %copy-start = (bf16[64,8,256]{2,1,0:T(8,128)(2,1)S(1)}, bf16[64,8,256]{2,1,0:T(8,128)(2,1)}, u32[]{:S(2)}) copy-start(bf16[64,8,256]{2,1,0:T(8,128)(2,1)} %param.8) | copy-start | bytes 786436
  138.5 21.2 %copy-start.3 = (f32[8,256]{1,0:T(8,128)S(1)}, f32[8,256]{1,0:T(8,128)}, u32[]{:S(2)}) copy-start(f32[8,256]{1,0:T(8,128)} %param.9) | copy-start | bytes 24580
  138.6 5.3 %collective-permute-start.4 = (f32[64,1,256]{2,1,0:T(1,128)S(1)}, f32[64,1,256]{2,1,0:T(1,128)S(1)}, u32[]{:S(2)}, u32[]{:S(2)}) collective-permute-start(f32[64,1,256]{2,1,0:T(1,128)S(1)} %get-tuple-element.14), channel_id=1, source_target_pairs={{8,0},{16,8},{24,16},{32,24},{40,32},{48,40},{56,48},{64,56},{72,6... | collective-permute-start | bytes 196616 | tf_op jit(solution)/shard_map/ppermute | solution.py:18
  139.9 5.3 %collective-permute-start.5 = (f32[64,1,256]{2,1,0:T(1,128)S(1)}, f32[64,1,256]{2,1,0:T(1,128)S(1)}, u32[]{:S(2)}, u32[]{:S(2)}) collective-permute-start(f32[64,1,256]{2,1,0:T(1,128)S(1)} %get-tuple-element.13), channel_id=1, source_target_pairs={{0,8},{8,16},{16,24},{24,32},{32,40},{40,48},{48,56},{56,64},{64,7... | collective-permute-start | bytes 196616 | tf_op jit(solution)/shard_map/ppermute | solution.py:15
  145.6 10.5 %collective-permute-start.6 = (f32[64,10,1]{2,1,0:T(8,128)S(1)}, f32[64,10,1]{2,1,0:T(8,128)S(1)}, u32[]{:S(2)}, u32[]{:S(2)}) collective-permute-start(f32[64,10,1]{2,1,0:T(8,128)S(1)} %get-tuple-element.9), channel_id=1, source_target_pairs={{1,0},{2,1},{3,2},{4,3},{5,4},{6,5},{7,6},{9,8},{10,9},{11,10},{12... | collective-permute-start | bytes 7688 | tf_op jit(solution)/shard_map/ppermute | solution.py:18
  151.7 8.0 %collective-permute-start.7 = (f32[64,10,1]{2,1,0:T(8,128)S(1)}, f32[64,10,1]{2,1,0:T(8,128)S(1)}, u32[]{:S(2)}, u32[]{:S(2)}) collective-permute-start(f32[64,10,1]{2,1,0:T(8,128)S(1)} %get-tuple-element.10), channel_id=1, source_target_pairs={{0,1},{1,2},{2,3},{3,4},{4,5},{5,6},{6,7},{8,9},{9,10},{10,11},{11... | collective-permute-start | bytes 7688 | tf_op jit(solution)/shard_map/ppermute | solution.py:15
Sparse Core Ops, SparseCore 0:
  32.8 38.8 all-gather.3
  93.2 43.9 reduce-scatter.1
  162.0 222.6 all-gather.5
